TPU v7x, 256 devices: a whole 4x4x8 slice. The times are simulated.
256 devices in a mesh: lon: 32 (over z, y_hi, core), lat: 8 (over y_lo, x).
Axes of the slice: x: 4, y: 4 (y_hi: 2, y_lo: 2; y = y_hi * 2 + y_lo), z: 8, core: 2. Of those that a mesh axis runs over, the one named last changes fastest.
Arguments:
- state: bfloat16 [360, 768, 128], P('lat', 'lon'), may hold values from -6 to 6
- land_sea: int32 [360, 768], P('lat', 'lon'), may hold values 0 or 1
- cotangent: bfloat16 [360, 768, 128], P('lat', 'lon'), may hold values from -6 to 6
- dw_kernel: bfloat16 [2, 7, 7, 128], replicated, may hold values from -0.875 to 0.875
- conv_bias: float32 [2, 128], replicated, may hold values from -3 to 3
- norm_gain: float32 [2, 128], replicated, may hold values from 0.1 to 1.9
- norm_bias: float32 [2, 128], replicated, may hold values from -3 to 3
- weight_in: bfloat16 [2, 128, 512], replicated, may hold values from -0.5 to 0.5
- bias_in: float32 [2, 512], replicated, may hold values from -3 to 3
- weight_out: bfloat16 [2, 512, 128], replicated, may hold values from -0.25 to 0.25
- bias_out: float32 [2, 128], replicated, may hold values from -3 to 3
- layer_scale: float32 [2, 128], replicated, may hold values from 0.3 to 1
Outputs:
- output: bfloat16 [360, 768, 128], P('lat', 'lon')
- grad_state: bfloat16 [360, 768, 128], P('lat', 'lon')
- grad_dw_kernel: float32 [2, 7, 7, 128], replicated
- grad_conv_bias: float32 [2, 128], replicated
- grad_norm_gain: float32 [2, 128], replicated
- grad_norm_bias: float32 [2, 128], replicated
- grad_weight_in: float32 [2, 128, 512], replicated
- grad_bias_in: float32 [2, 512], replicated
- grad_weight_out: float32 [2, 512, 128], replicated
- grad_bias_out: float32 [2, 128], replicated
- grad_layer_scale: float32 [2, 128], replicated
All inputs are finite; a program needn't handle non-finite values. No bound on the sum of `land_sea` on one device may be relied on, other than what follows from the above.
Results may differ from a plain program's by a relative error of at most 0.02.
Values may be sent and summed in bfloat16 or wider, within the bound.
A program may use at most 64 MiB of HBM per device.

v0:
```python
import math
import jax
import jax.numpy as jnp
from jax import lax
from jax.sharding import PartitionSpec as P

KSIZE = 7
BLOCKS = 2
EPS_NORM = 1e-06
INV_ROOT_TWO = 0.7071067811865476
INV_ROOT_TWO_PI = 0.3989422804014327


def with_halo(shard, sides, width, wrap):
    for axis, dim in sides:
        count, length = (lax.axis_size(axis), shard.shape[dim])
        up = [(i, (i + 1) % count) for i in range(count if wrap else count - 1)]
        down = [(j, i) for i, j in up]
        last = lax.slice_in_dim(shard, length - width, length, axis=dim)
        first = lax.slice_in_dim(shard, 0, width, axis=dim)
        before = lax.ppermute(last, axis, up)
        after = lax.ppermute(first, axis, down)
        shard = jnp.concatenate([before, shard, after], axis=dim)
    return shard


def depthwise(window, kernel, height, breadth):
    summed = jnp.zeros((height, breadth, window.shape[2]), jnp.float32)
    for tap_row in range(KSIZE):
        for tap_col in range(KSIZE):
            piece = window[tap_row : tap_row + height, tap_col : tap_col + breadth].astype(
                jnp.float32
            )
            summed = summed + piece * kernel[tap_row, tap_col].astype(jnp.float32)
    return summed


def block_forward(window, land_rows, params):
    (
        kernel,
        conv_bias,
        norm_gain,
        norm_bias,
        weight_in,
        bias_in,
        weight_out,
        bias_out,
        layer_scale,
    ) = params
    margin = KSIZE // 2
    height = window.shape[0] - 2 * margin
    breadth = window.shape[1] - 2 * margin
    channels = window.shape[2]
    cell_count = height * breadth
    mixed_sum = depthwise(window, kernel, height, breadth) + conv_bias
    center = mixed_sum - jnp.mean(mixed_sum, axis=-1, keepdims=True)
    inverse = lax.rsqrt(jnp.mean(center * center, axis=-1, keepdims=True) + EPS_NORM)
    normed = (center * inverse).reshape(cell_count, channels)
    lifted = (normed * norm_gain + norm_bias).astype(jnp.bfloat16)
    hidden = jnp.dot(lifted, weight_in, preferred_element_type=jnp.float32) + bias_in
    active = jax.nn.gelu(hidden, approximate=False).astype(jnp.bfloat16)
    branch = jnp.dot(active, weight_out, preferred_element_type=jnp.float32) + bias_out
    interior = (
        window[margin : margin + height, margin : margin + breadth]
        .astype(jnp.float32)
        .reshape(cell_count, channels)
    )
    ocean_mask = land_rows.reshape(cell_count, 1).astype(jnp.float32)
    result = (
        ((interior + layer_scale * branch) * ocean_mask)
        .astype(jnp.bfloat16)
        .reshape(height, breadth, channels)
    )
    return (result, (normed, inverse.reshape(cell_count, 1), lifted, hidden, active, branch))


def block_backward(window, land_rows, incoming, params, stored):
    (
        kernel,
        conv_bias,
        norm_gain,
        norm_bias,
        weight_in,
        bias_in,
        weight_out,
        bias_out,
        layer_scale,
    ) = params
    normed, inverse, lifted, hidden, active, branch = stored
    margin = KSIZE // 2
    height = window.shape[0] - 2 * margin
    breadth = window.shape[1] - 2 * margin
    channels = window.shape[2]
    cell_count = height * breadth
    ocean_mask = land_rows.reshape(cell_count, 1).astype(jnp.float32)
    masked = incoming.reshape(cell_count, channels).astype(jnp.float32) * ocean_mask
    grad_branch = (masked * layer_scale).astype(jnp.bfloat16)
    contract_rows = (((0,), (0,)), ((), ()))
    contract_cols = (((1,), (1,)), ((), ()))
    grad_scale = jnp.sum(masked * branch, axis=0)
    grad_bias_out = jnp.sum(grad_branch.astype(jnp.float32), axis=0)
    grad_weight_out = lax.dot_general(
        active, grad_branch, contract_rows, preferred_element_type=jnp.float32
    )
    grad_active = lax.dot_general(
        grad_branch, weight_out, contract_cols, preferred_element_type=jnp.float32
    )
    cumulative = 0.5 * (1.0 + lax.erf(hidden * INV_ROOT_TWO))
    density = jnp.exp(-0.5 * hidden * hidden) * INV_ROOT_TWO_PI
    grad_hidden = (grad_active * (cumulative + hidden * density)).astype(jnp.bfloat16)
    grad_bias_in = jnp.sum(grad_hidden.astype(jnp.float32), axis=0)
    grad_weight_in = lax.dot_general(
        lifted, grad_hidden, contract_rows, preferred_element_type=jnp.float32
    )
    grad_lifted = lax.dot_general(
        grad_hidden, weight_in, contract_cols, preferred_element_type=jnp.float32
    )
    grad_gain = jnp.sum(grad_lifted * normed, axis=0)
    grad_shift = jnp.sum(grad_lifted, axis=0)
    scaled = grad_lifted * norm_gain
    grad_mixed = inverse * (
        scaled
        - jnp.mean(scaled, axis=-1, keepdims=True)
        - normed * jnp.mean(scaled * normed, axis=-1, keepdims=True)
    )
    grad_mixed = grad_mixed.astype(jnp.bfloat16).reshape(height, breadth, channels)
    spread = grad_mixed.astype(jnp.float32)
    grad_conv_bias = jnp.sum(spread, axis=(0, 1))
    tap_sums = []
    for tap_row in range(KSIZE):
        for tap_col in range(KSIZE):
            piece = window[tap_row : tap_row + height, tap_col : tap_col + breadth].astype(
                jnp.float32
            )
            tap_sums.append(jnp.sum(spread * piece, axis=(0, 1)))
    grad_kernel = jnp.stack(tap_sums).reshape(KSIZE, KSIZE, channels)
    gradients = (
        grad_kernel,
        grad_conv_bias,
        grad_gain,
        grad_shift,
        grad_weight_in,
        grad_bias_in,
        grad_weight_out,
        grad_bias_out,
        grad_scale,
    )
    return (grad_mixed, masked.reshape(height, breadth, channels), gradients)


def adjoint(padded, masked, kernel):
    margin = KSIZE // 2
    height = masked.shape[0]
    breadth = masked.shape[1]
    summed = masked
    for tap_row in range(KSIZE):
        for tap_col in range(KSIZE):
            first_row = 2 * margin - tap_row
            first_col = 2 * margin - tap_col
            piece = padded[first_row : first_row + height, first_col : first_col + breadth].astype(
                jnp.float32
            )
            summed = summed + piece * kernel[tap_row, tap_col].astype(jnp.float32)
    return summed.astype(jnp.bfloat16)


def extend(tile_field):
    beside_all = with_halo(tile_field, (("lon", 1),), KSIZE // 2, True)
    return with_halo(beside_all, (("lat", 0),), KSIZE // 2, False)


def sum_everything(parts):
    (
        kernel_part,
        conv_part,
        gain_part,
        shift_part,
        first_part,
        first_bias,
        second_part,
        second_bias,
        scale_part,
    ) = parts
    return lax.psum(
        (
            kernel_part,
            conv_part,
            gain_part,
            shift_part,
            first_part,
            first_bias,
            second_part,
            second_bias,
            scale_part,
        ),
        ("lon", "lat"),
    )


def on_device(
    state,
    land_sea,
    cotangent,
    dw_kernel,
    conv_bias,
    norm_gain,
    norm_bias,
    weight_in,
    bias_in,
    weight_out,
    bias_out,
    layer_scale,
):
    stacked = (
        dw_kernel,
        conv_bias,
        norm_gain,
        norm_bias,
        weight_in,
        bias_in,
        weight_out,
        bias_out,
        layer_scale,
    )
    height = state.shape[0]
    breadth = state.shape[1]
    grad_norm = 1.0 / math.sqrt(lax.axis_size("lat") * height * lax.axis_size("lon") * breadth)
    current = state
    windows = []
    stored_all = []
    for layer_index in range(BLOCKS):
        params = tuple((member[layer_index] for member in stacked))
        window = extend(current)
        windows.append(window)
        outcome = block_forward(window, land_sea, params)
        current = outcome[0]
        stored_all.append(outcome[1])
    incoming = cotangent
    per_layer = [None] * BLOCKS
    for layer_index in reversed(range(BLOCKS)):
        params = tuple((member[layer_index] for member in stacked))
        stored = stored_all[layer_index]
        grad_mixed, masked, gradients = block_backward(
            windows[layer_index], land_sea, incoming, params, stored
        )
        incoming = adjoint(extend(grad_mixed), masked, params[0])
        per_layer[layer_index] = gradients
    combined = tuple(
        (
            jnp.stack([per_layer[layer_index][member] for layer_index in range(BLOCKS)])
            for member in range(9)
        )
    )
    combined = sum_everything(combined)
    scaled = [member * grad_norm for member in combined]
    return (
        current,
        incoming,
        scaled[0],
        scaled[1],
        scaled[2],
        scaled[3],
        scaled[4],
        scaled[5],
        scaled[6],
        scaled[7],
        scaled[8],
    )


def solution(mesh):
    placed = (
        P("lat", "lon", None),
        P("lat", "lon"),
        P("lat", "lon", None),
        P(),
        P(),
        P(),
        P(),
        P(),
        P(),
        P(),
        P(),
        P(),
    )
    return jax.shard_map(
        on_device,
        mesh=mesh,
        in_specs=placed,
        out_specs=(
            P("lat", "lon", None),
            P("lat", "lon", None),
            P(),
            P(),
            P(),
            P(),
            P(),
            P(),
            P(),
            P(),
            P(),
        ),
        check_vma=False,
    )
```

profile of v0, /device:TPU:2, one launch (start us, length us, event | category | flops | bytes accessed | tf_op | source)
XLA Modules:
  0.0 509.7 jit_solution(3118116453118885206)
XLA Ops:
  8.3 8.0 %collective-permute-start.1 = (bf16[45,3,128]{2,1,0:T(4,128)(2,1)S(1)}, bf16[45,3,128]{2,1,0:T(4,128)(2,1)S(1)}, u32[]{:S(2)}, u32[]{:S(2)}) collective-permute-start(bf16[45,3,128]{2,1,0:T(4,128)(2,1)S(1)} %get-tuple-element.208), channel_id=1, source_target_pairs={{8,0},{16,8},{24,16},{32,24},{40,32},{48,40},{56,48},{64,56},{72,6... | collective-permute-start | bytes 103688 | tf_op jit(solution)/shard_map/ppermute | solution.py:22
  24.9 2.5 convert_reduce_fusion.3
  29.2 3.4 collective-permute-start.2
  32.6 2.4 collective-permute-start.3
  35.1 3.2 collective-permute-done.3
  38.6 5.0 fusion.421
  44.7 6.0 %fusion.4 = (bf16[1080,512]{1,0:T(8,128)(2,1)S(1)}, f32[1080,512]{1,0:T(8,128)}) fusion(f32[512]{0:T(512)S(1)} %bitcast.782, bf16[1080,128]{1,0:T(8,128)(2,1)S(1)} %bitcast.742, bf16[2,128,512]{2,1,0:T(8,128)(2,1)S(1)} %copy-done.11), kind=kOutput, calls=%fused_computation.113 | convolution fusion | flops 178053120 | bytes 3727360 | tf_op jit(solution)/shard_map/dot_general | solution.py:60
  53.2 5.3 %collective-permute-start.5 = (bf16[45,3,128]{2,1,0:T(4,128)(2,1)S(1)}, bf16[45,3,128]{2,1,0:T(4,128)(2,1)S(1)}, u32[]{:S(2)}, u32[]{:S(2)}) collective-permute-start(bf16[45,3,128]{2,1,0:T(4,128)(2,1)S(1)} %get-tuple-element.206), channel_id=1, source_target_pairs={{8,0},{16,8},{24,16},{32,24},{40,32},{48,40},{56,48},{64,56},{72,6... | collective-permute-start | bytes 103688 | tf_op jit(solution)/shard_map/ppermute | solution.py:22
  60.3 3.1 collective-permute-start.6
  63.4 3.1 collective-permute-start.7
  66.8 3.1 collective-permute-done.7
  70.1 5.0 fusion.419
  78.7 7.0 %fusion.7 = (bf16[1080,512]{1,0:T(8,128)(2,1)}, f32[1080,512]{1,0:T(8,128)S(1)}) fusion(f32[512]{0:T(512)} %bitcast.780, bf16[1080,128]{1,0:T(8,128)(2,1)S(1)} %bitcast.741, bf16[2,128,512]{2,1,0:T(8,128)(2,1)} %param.19), kind=kOutput, calls=%fused_computation.116 | convolution fusion | flops 178053120 | bytes 3727360 | tf_op jit(solution)/shard_map/dot_general | solution.py:60
  85.7 1.9 convert_reduce_fusion
  93.1 5.3 %collective-permute-start.9 = (bf16[45,3,128]{2,1,0:T(4,128)(2,1)S(1)}, bf16[45,3,128]{2,1,0:T(4,128)(2,1)S(1)}, u32[]{:S(2)}, u32[]{:S(2)}) collective-permute-start(bf16[45,3,128]{2,1,0:T(4,128)(2,1)S(1)} %get-tuple-element.204), channel_id=1, source_target_pairs={{8,0},{16,8},{24,16},{32,24},{40,32},{48,40},{56,48},{64,56},{72,6... | collective-permute-start | bytes 103688 | tf_op jit(solution)/shard_map/ppermute | solution.py:22
  98.4 1.7 fusion.200
  100.4 2.2 collective-permute-start.10
  102.6 12.7 %collective-permute-start.11 = (bf16[3,30,128]{2,1,0:T(8,128)(2,1)S(1)}, bf16[3,30,128]{2,1,0:T(8,128)(2,1)S(1)}, u32[]{:S(2)}, u32[]{:S(2)}) collective-permute-start(bf16[3,30,128]{2,1,0:T(8,128)(2,1)S(1)} %get-tuple-element.191), channel_id=1, source_target_pairs={{0,1},{1,2},{2,3},{3,4},{4,5},{5,6},{6,7},{8,9},{9,10},{10,11},{11... | collective-permute-start | bytes 69128 | tf_op jit(solution)/shard_map/ppermute | solution.py:21
  115.8 4.9 stack.474
  122.0 6.2 %multiply_convert_fusion.1 = (bf16[1080,128]{1,0:T(8,128)(2,1)S(1)}, bf16[45,24,128]{2,1,0:T(8,128)(2,1)S(1)}) fusion(f32[1080]{0:T(1024)S(1)} %convert_element_type.1163, f32[128]{0:T(128)S(1)} %copy-done.21, f32[128]{0:T(128)S(1)} %copy-done.102, bf16[48,30,128]{2,1,0:T(8,128)(2,1)S(1)} %get-tuple-element.189, f32[128]{0:T(128)S(1)} %copy-done.104, ...), kind=kLoop, calls=%fused_computation.516 | loop fusion | flops 23777280 | bytes 12821440 | tf_op jit(solution)/shard_map/convert_element_type | solution.py:97
  128.5 1.9 convert_reduce_fusion.1
  133.0 1.6 fusion.247
  134.6 1.6 fusion.275
  137.5 2.4 multiply_reduce_fusion.1
  143.8 81.3 %all-reduce = (f32[2,7,7,128]{3,2,1,0:T(8,128)S(1)}, f32[2,128]{1,0:T(2,128)S(1)}, f32[2,128]{1,0:T(2,128)S(1)}, f32[2,128]{1,0:T(2,128)S(1)}, f32[2,512]{1,0:T(...) all-reduce(f32[2,7,7,128]{3,2,1,0:T(8,128)S(1)} %pad_maximum_fusion, ...), channel_id=1, replica_groups=mesh['lon'=32,'lat'=8] {'lon','lat'}, use_global_device_ids=true, to_apply=%region_106.0 | all-reduce | flops 14848 | bytes 118784 | tf_op jit(solution)/shard_map/psum | solution.py:184
  230.7 6.0 %collective-permute-done.12 = bf16[45,3,128]{2,1,0:T(4,128)(2,1)S(1)} collective-permute-done((bf16[45,3,128]{2,1,0:T(4,128)(2,1)S(1)}, bf16[45,3,128]{2,1,0:T(4,128)(2,1)S(1)}, u32[]{:S(2)}, u32[]{:S(2)}) %collective-permute-start.12) | collective-permute-done | bytes 34592 | tf_op jit(solution)/shard_map/ppermute | solution.py:21
  236.7 2.6 collective-permute-start.14
  239.3 3.2 collective-permute-start.15
  245.6 5.8 %fusion.280 = bf16[45,24,128]{2,1,0:T(8,128)(2,1)} fusion(bf16[45,24,128]{2,1,0:T(8,128)(2,1)S(1)} %bitcast.724, bf16[45,24,128]{2,1,0:T(8,128)(2,1)S(1)} %get-tuple-element.167, bf16[45,3,128]{2,1,0:T(4,128)(2,1)S(1)} %collective-permute-done.12, bf16[45,3,128]{2,1,0:T(4,128)(2,1)S(1)} %collective-permute-done.13, ...), kind=kLoop, calls=%fused_computation.534 | loop fusion | flops 23224320 | bytes 12540128 | tf_op jit(solution)/shard_map/convert_element_type | solution.py:164
  251.4 247.4 %all-reduce.4.cloned.1.call-done = (f32[2,128,512]{2,1,0:T(8,128)}, f32[2,512,128]{2,1,0:T(8,128)}) async-done(((f32[2,128,512]{2,1,0:T(8,128)}, f32[2,512,128]{2,1,0:T(8,128)}), (f32[2,128,512]{2,1,0:T(8,128)}, f32[2,512,128]{2,1,0:T(8,128)})) %all-reduce.4.cloned.1.call-update) | async-done | bytes 1048592 | tf_op jit(solution)/shard_map/psum | solution.py:184
  498.8 1.9 broadcast_multiply_fusion.1
  500.7 1.9 broadcast_multiply_fusion
  (468 shorter events, 42.6 us)
Async XLA Ops:
  7.2 31.2 %copy-start = (bf16[45,24,128]{2,1,0:T(8,128)(2,1)S(1)}, bf16[45,24,128]{2,1,0:T(8,128)(2,1)}, u32[]{:S(2)}) copy-start(bf16[45,24,128]{2,1,0:T(8,128)(2,1)} %param.12) | copy-start | bytes 829444
  7.2 491.6 %all-reduce.4.cloned.1.call-start = ((), (), s32[]{:S(2)}) async-start(), calls=%async_computation | async-start | bytes 2097152 | tf_op jit(solution)/shard_map/psum | solution.py:184
  8.2 20.2 %collective-permute-start = (bf16[45,3,128]{2,1,0:T(4,128)(2,1)S(1)}, bf16[45,3,128]{2,1,0:T(4,128)(2,1)S(1)}, u32[]{:S(2)}, u32[]{:S(2)}) collective-permute-start(bf16[45,3,128]{2,1,0:T(4,128)(2,1)S(1)} %get-tuple-element.207), channel_id=1, source_target_pairs={{0,8},{8,16},{16,24},{24,32},{32,40},{40,48},{48,56},{56,64},{64,7... | collective-permute-start | bytes 103688 | tf_op jit(solution)/shard_map/ppermute | solution.py:21
  8.3 20.1 %collective-permute-start.1 = (bf16[45,3,128]{2,1,0:T(4,128)(2,1)S(1)}, bf16[45,3,128]{2,1,0:T(4,128)(2,1)S(1)}, u32[]{:S(2)}, u32[]{:S(2)}) collective-permute-start(bf16[45,3,128]{2,1,0:T(4,128)(2,1)S(1)} %get-tuple-element.208), channel_id=1, source_target_pairs={{8,0},{16,8},{24,16},{32,24},{40,32},{48,40},{56,48},{64,56},{72,6... | collective-permute-start | bytes 103688 | tf_op jit(solution)/shard_map/ppermute | solution.py:22
  17.2 26.3 %copy-start.25 = (f32[128]{0:T(128)}, f32[128]{0:T(128)S(1)}, u32[]{:S(2)}) copy-start(f32[128]{0:T(128)S(1)} %get-tuple-element.298) | copy-start | bytes 1540
  17.2 26.3 %copy-start.27 = (f32[128]{0:T(128)}, f32[128]{0:T(128)S(1)}, u32[]{:S(2)}) copy-start(f32[128]{0:T(128)S(1)} %get-tuple-element.299) | copy-start | bytes 1540
  17.3 26.3 %copy-start.29 = (f32[128]{0:T(128)}, f32[128]{0:T(128)S(1)}, u32[]{:S(2)}) copy-start(f32[128]{0:T(128)S(1)} %get-tuple-element.300) | copy-start | bytes 1540
  17.3 26.3 %copy-start.31 = (f32[128]{0:T(128)}, f32[128]{0:T(128)S(1)}, u32[]{:S(2)}) copy-start(f32[128]{0:T(128)S(1)} %get-tuple-element.301) | copy-start | bytes 1540
  17.3 26.3 %copy-start.33 = (f32[128]{0:T(128)}, f32[128]{0:T(128)S(1)}, u32[]{:S(2)}) copy-start(f32[128]{0:T(128)S(1)} %get-tuple-element.302) | copy-start | bytes 1540
  17.3 26.3 %copy-start.35 = (f32[128]{0:T(128)}, f32[128]{0:T(128)S(1)}, u32[]{:S(2)}) copy-start(f32[128]{0:T(128)S(1)} %get-tuple-element.303) | copy-start | bytes 1540
  17.3 26.3 %copy-start.37 = (f32[128]{0:T(128)}, f32[128]{0:T(128)S(1)}, u32[]{:S(2)}) copy-start(f32[128]{0:T(128)S(1)} %get-tuple-element.304) | copy-start | bytes 1540
  17.3 26.3 %copy-start.39 = (f32[128]{0:T(128)}, f32[128]{0:T(128)S(1)}, u32[]{:S(2)}) copy-start(f32[128]{0:T(128)S(1)} %get-tuple-element.305) | copy-start | bytes 1540
  17.3 26.3 %copy-start.41 = (f32[128]{0:T(128)}, f32[128]{0:T(128)S(1)}, u32[]{:S(2)}) copy-start(f32[128]{0:T(128)S(1)} %get-tuple-element.306) | copy-start | bytes 1540
  17.3 26.3 %copy-start.43 = (f32[128]{0:T(128)}, f32[128]{0:T(128)S(1)}, u32[]{:S(2)}) copy-start(f32[128]{0:T(128)S(1)} %get-tuple-element.307) | copy-start | bytes 1540
  17.3 26.3 %copy-start.45 = (f32[128]{0:T(128)}, f32[128]{0:T(128)S(1)}, u32[]{:S(2)}) copy-start(f32[128]{0:T(128)S(1)} %get-tuple-element.308) | copy-start | bytes 1540
  17.4 26.3 %copy-start.47 = (f32[128]{0:T(128)}, f32[128]{0:T(128)S(1)}, u32[]{:S(2)}) copy-start(f32[128]{0:T(128)S(1)} %get-tuple-element.279) | copy-start | bytes 1540
  29.2 5.9 %collective-permute-start.2 = (bf16[3,30,128]{2,1,0:T(8,128)(2,1)S(1)}, bf16[3,30,128]{2,1,0:T(8,128)(2,1)S(1)}, u32[]{:S(2)}, u32[]{:S(2)}) collective-permute-start(bf16[3,30,128]{2,1,0:T(8,128)(2,1)S(1)} %get-tuple-element.198), channel_id=1, source_target_pairs={{0,1},{1,2},{2,3},{3,4},{4,5},{5,6},{6,7},{8,9},{9,10},{10,11},{11... | collective-permute-start | bytes 69128 | tf_op jit(solution)/shard_map/ppermute | solution.py:21
  32.6 5.7 %collective-permute-start.3 = (bf16[3,30,128]{2,1,0:T(8,128)(2,1)S(1)}, bf16[3,30,128]{2,1,0:T(8,128)(2,1)S(1)}, u32[]{:S(2)}, u32[]{:S(2)}) collective-permute-start(bf16[3,30,128]{2,1,0:T(8,128)(2,1)S(1)} %get-tuple-element.199), channel_id=1, source_target_pairs={{1,0},{2,1},{3,2},{4,3},{5,4},{6,5},{7,6},{9,8},{10,9},{11,10},{12... | collective-permute-start | bytes 69128 | tf_op jit(solution)/shard_map/ppermute | solution.py:22
  53.1 7.2 %collective-permute-start.4 = (bf16[45,3,128]{2,1,0:T(4,128)(2,1)S(1)}, bf16[45,3,128]{2,1,0:T(4,128)(2,1)S(1)}, u32[]{:S(2)}, u32[]{:S(2)}) collective-permute-start(bf16[45,3,128]{2,1,0:T(4,128)(2,1)S(1)} %get-tuple-element.205), channel_id=1, source_target_pairs={{0,8},{8,16},{16,24},{24,32},{32,40},{40,48},{48,56},{56,64},{64,7... | collective-permute-start | bytes 103688 | tf_op jit(solution)/shard_map/ppermute | solution.py:21
  53.2 7.1 %collective-permute-start.5 = (bf16[45,3,128]{2,1,0:T(4,128)(2,1)S(1)}, bf16[45,3,128]{2,1,0:T(4,128)(2,1)S(1)}, u32[]{:S(2)}, u32[]{:S(2)}) collective-permute-start(bf16[45,3,128]{2,1,0:T(4,128)(2,1)S(1)} %get-tuple-element.206), channel_id=1, source_target_pairs={{8,0},{16,8},{24,16},{32,24},{40,32},{48,40},{56,48},{64,56},{72,6... | collective-permute-start | bytes 103688 | tf_op jit(solution)/shard_map/ppermute | solution.py:22
  60.3 6.5 %collective-permute-start.6 = (bf16[3,30,128]{2,1,0:T(8,128)(2,1)S(1)}, bf16[3,30,128]{2,1,0:T(8,128)(2,1)S(1)}, u32[]{:S(2)}, u32[]{:S(2)}) collective-permute-start(bf16[3,30,128]{2,1,0:T(8,128)(2,1)S(1)} %get-tuple-element.194), channel_id=1, source_target_pairs={{0,1},{1,2},{2,3},{3,4},{4,5},{5,6},{6,7},{8,9},{9,10},{10,11},{11... | collective-permute-start | bytes 69128 | tf_op jit(solution)/shard_map/ppermute | solution.py:21
  63.4 6.4 %collective-permute-start.7 = (bf16[3,30,128]{2,1,0:T(8,128)(2,1)S(1)}, bf16[3,30,128]{2,1,0:T(8,128)(2,1)S(1)}, u32[]{:S(2)}, u32[]{:S(2)}) collective-permute-start(bf16[3,30,128]{2,1,0:T(8,128)(2,1)S(1)} %get-tuple-element.195), channel_id=1, source_target_pairs={{1,0},{2,1},{3,2},{4,3},{5,4},{6,5},{7,6},{9,8},{10,9},{11,10},{12... | collective-permute-start | bytes 69128 | tf_op jit(solution)/shard_map/ppermute | solution.py:22
  93.0 7.3 %collective-permute-start.8 = (bf16[45,3,128]{2,1,0:T(4,128)(2,1)S(1)}, bf16[45,3,128]{2,1,0:T(4,128)(2,1)S(1)}, u32[]{:S(2)}, u32[]{:S(2)}) collective-permute-start(bf16[45,3,128]{2,1,0:T(4,128)(2,1)S(1)} %get-tuple-element.203), channel_id=1, source_target_pairs={{0,8},{8,16},{16,24},{24,32},{32,40},{40,48},{48,56},{56,64},{64,7... | collective-permute-start | bytes 103688 | tf_op jit(solution)/shard_map/ppermute | solution.py:21
  93.1 7.3 %collective-permute-start.9 = (bf16[45,3,128]{2,1,0:T(4,128)(2,1)S(1)}, bf16[45,3,128]{2,1,0:T(4,128)(2,1)S(1)}, u32[]{:S(2)}, u32[]{:S(2)}) collective-permute-start(bf16[45,3,128]{2,1,0:T(4,128)(2,1)S(1)} %get-tuple-element.204), channel_id=1, source_target_pairs={{8,0},{16,8},{24,16},{32,24},{40,32},{48,40},{56,48},{64,56},{72,6... | collective-permute-start | bytes 103688 | tf_op jit(solution)/shard_map/ppermute | solution.py:22
  100.4 20.3 %collective-permute-start.10 = (bf16[3,30,128]{2,1,0:T(8,128)(2,1)S(1)}, bf16[3,30,128]{2,1,0:T(8,128)(2,1)S(1)}, u32[]{:S(2)}, u32[]{:S(2)}) collective-permute-start(bf16[3,30,128]{2,1,0:T(8,128)(2,1)S(1)} %get-tuple-element.190), channel_id=1, source_target_pairs={{1,0},{2,1},{3,2},{4,3},{5,4},{6,5},{7,6},{9,8},{10,9},{11,10},{12... | collective-permute-start | bytes 69128 | tf_op jit(solution)/shard_map/ppermute | solution.py:22
  102.6 18.2 %collective-permute-start.11 = (bf16[3,30,128]{2,1,0:T(8,128)(2,1)S(1)}, bf16[3,30,128]{2,1,0:T(8,128)(2,1)S(1)}, u32[]{:S(2)}, u32[]{:S(2)}) collective-permute-start(bf16[3,30,128]{2,1,0:T(8,128)(2,1)S(1)} %get-tuple-element.191), channel_id=1, source_target_pairs={{0,1},{1,2},{2,3},{3,4},{4,5},{5,6},{6,7},{8,9},{9,10},{10,11},{11... | collective-permute-start | bytes 69128 | tf_op jit(solution)/shard_map/ppermute | solution.py:21
  140.7 87.8 %copy-start.18 = (bf16[45,3,128]{2,1,0:T(4,128)(2,1)S(1)}, bf16[45,3,128]{2,1,0:T(4,128)(2,1)}, u32[]{:S(2)}) copy-start(bf16[45,3,128]{2,1,0:T(4,128)(2,1)} %get-tuple-element.201) | copy-start | bytes 103684
  140.8 101.8 %copy-start.6 = (f32[1,128,512]{2,1,0:T(8,128)S(1)}, f32[1,128,512]{2,1,0:T(8,128)}, u32[]{:S(2)}) copy-start(f32[1,128,512]{2,1,0:T(8,128)} %convolution_bitcast_fusion.3) | copy-start | bytes 786436
  228.6 2.1 collective-permute-start.13
  229.3 7.4 %collective-permute-start.12 = (bf16[45,3,128]{2,1,0:T(4,128)(2,1)S(1)}, bf16[45,3,128]{2,1,0:T(4,128)(2,1)S(1)}, u32[]{:S(2)}, u32[]{:S(2)}) collective-permute-start(bf16[45,3,128]{2,1,0:T(4,128)(2,1)S(1)} %get-tuple-element.202), channel_id=1, source_target_pairs={{0,8},{8,16},{16,24},{24,32},{32,40},{40,48},{48,56},{56,64},{64,7... | collective-permute-start | bytes 103688 | tf_op jit(solution)/shard_map/ppermute | solution.py:21
  236.7 7.4 %collective-permute-start.14 = (bf16[3,30,128]{2,1,0:T(8,128)(2,1)S(1)}, bf16[3,30,128]{2,1,0:T(8,128)(2,1)S(1)}, u32[]{:S(2)}, u32[]{:S(2)}) collective-permute-start(bf16[3,30,128]{2,1,0:T(8,128)(2,1)S(1)} %get-tuple-element.186), channel_id=1, source_target_pairs={{1,0},{2,1},{3,2},{4,3},{5,4},{6,5},{7,6},{9,8},{10,9},{11,10},{12... | collective-permute-start | bytes 69128 | tf_op jit(solution)/shard_map/ppermute | solution.py:22
  239.3 5.7 %collective-permute-start.15 = (bf16[3,30,128]{2,1,0:T(8,128)(2,1)S(1)}, bf16[3,30,128]{2,1,0:T(8,128)(2,1)S(1)}, u32[]{:S(2)}, u32[]{:S(2)}) collective-permute-start(bf16[3,30,128]{2,1,0:T(8,128)(2,1)S(1)} %get-tuple-element.187), channel_id=1, source_target_pairs={{0,1},{1,2},{2,3},{3,4},{4,5},{5,6},{6,7},{8,9},{9,10},{10,11},{11... | collective-permute-start | bytes 69128 | tf_op jit(solution)/shard_map/ppermute | solution.py:21
  (171 other events, 2235.0 us)
Sparse Core Ops, SparseCore 0:
  244.2 254.5 all-reduce.3
where the time goes:
time: 517 us; the launch traced here: 510 us
  waiting for transfers between devices  262 us (51%)
  blocking collectives  81.3 us (16%)
  starting transfers between devices  52.5 us (10%)
  other arithmetic  52.3 us (10%)
  matrix products  25.1 us (5%)
  local copies, waits for them, and re-layouts  18.7 us (4%)
  between operations  17.3 us (3%)
    psum x1, waiting for transfers between devices, sum_everything(): lax.psum((kernel_part, conv_part, gain_part, shift_part, first_part, firs...  247 us
    psum x1, blocking collectives, sum_everything(): lax.psum((kernel_part, conv_part, gain_part, shift_part, first_part, firs...  81.3 us
    ppermute x8, starting transfers between devices, with_halo(): after = lax.ppermute(first, axis, down)  29.4 us
    ppermute x8, starting transfers between devices, with_halo(): before = lax.ppermute(last, axis, up)  23 us
    dot_general x2, matrix products, block_forward(): jnp.dot(lifted, weight_in, preferred_element_type=jnp.float32) + bias_in  13 us
  transfers between devices with their start and end apart: 17, of which 7 were waited for; matrix products, arithmetic and copies ran while one was open for 5% of the time, Pallas kernels for 0%

commit v1 on v0

--- a/solution.py
+++ b/solution.py
@@ -3,12 +3,19 @@
 import jax.numpy as jnp
 from jax import lax
 from jax.sharding import PartitionSpec as P
+from jax.lax import psum
 
 KSIZE = 7
 BLOCKS = 2
 EPS_NORM = 1e-06
 INV_ROOT_TWO = 0.7071067811865476
 INV_ROOT_TWO_PI = 0.3989422804014327
+
+
+def extend_cells(s0):
+    for ii in ("lon", "lat"):
+        s0 = psum(s0, ii)
+    return s0
 
 
 def with_halo(shard, sides, width, wrap):
@@ -181,7 +188,7 @@
         second_bias,
         scale_part,
     ) = parts
-    return lax.psum(
+    return extend_cells(
         (
             kernel_part,
             conv_part,
@@ -192,8 +199,7 @@
             second_part,
             second_bias,
             scale_part,
-        ),
-        ("lon", "lat"),
+        )
     )
 
 

time: 517 us -> 690 us (1.33)
  waiting for transfers between devices: 262 us -> 348 us
  blocking collectives: 81.3 us -> 166 us
    psum x1 -> x2, waiting for transfers between devices: 247 us -> 336 us  [extend_cells(): s0 = psum(s0, ii)]
    psum x1 -> x2, blocking collectives: 81.3 us -> 166 us  [extend_cells(): s0 = psum(s0, ii)]
  transfers between devices with their start and end apart: 17 -> 18, of which waited for: 7 -> 7; matrix products, arithmetic and copies ran while one was open for 5% -> 4% of each run, Pallas kernels for 0% -> 0%
where the time goes in v1:
time: 690 us; the launch traced here: 681 us
  waiting for transfers between devices  348 us (50%)
  blocking collectives  166 us (24%)
  starting transfers between devices  54.6 us (8%)
  other arithmetic  52.3 us (8%)
  matrix products  24.7 us (4%)
  local copies, waits for them, and re-layouts  18 us (3%)
  between operations  17.4 us (3%)
    psum x2, waiting for transfers between devices, extend_cells(): s0 = psum(s0, ii)  336 us
    psum x2, blocking collectives, extend_cells(): s0 = psum(s0, ii)  166 us
    ppermute x8, starting transfers between devices, with_halo(): after = lax.ppermute(first, axis, down)  30.6 us
    ppermute x8, starting transfers between devices, with_halo(): before = lax.ppermute(last, axis, up)  23.9 us
  transfers between devices with their start and end apart: 18, of which 7 were waited for; matrix products, arithmetic and copies ran while one was open for 4% of the time, Pallas kernels for 0%

profile of v1, /device:TPU:2, one launch (start us, length us, event | category | flops | bytes accessed | tf_op | source)
XLA Modules:
  0.0 681.0 jit_solution(319241393124355971)
XLA Ops:
  8.3 8.0 %collective-permute-start.1 = (bf16[45,3,128]{2,1,0:T(4,128)(2,1)S(1)}, bf16[45,3,128]{2,1,0:T(4,128)(2,1)S(1)}, u32[]{:S(2)}, u32[]{:S(2)}) collective-permute-start(bf16[45,3,128]{2,1,0:T(4,128)(2,1)S(1)} %get-tuple-element.217), channel_id=1, source_target_pairs={{8,0},{16,8},{24,16},{32,24},{40,32},{48,40},{56,48},{64,56},{72,6... | collective-permute-start | bytes 103688 | tf_op jit(solution)/shard_map/ppermute | solution.py:29
  24.9 2.5 convert_reduce_fusion.3
  29.2 3.4 collective-permute-start.2
  32.6 2.4 collective-permute-start.3
  35.1 3.2 collective-permute-done.3
  38.6 5.0 fusion.421
  44.7 6.0 fusion.4
  53.2 5.3 collective-permute-start.5
  60.3 3.1 collective-permute-start.6
  63.4 3.1 collective-permute-start.7
  66.8 3.1 collective-permute-done.7
  70.1 5.0 fusion.419
  78.7 7.0 %fusion.7 = (bf16[1080,512]{1,0:T(8,128)(2,1)}, f32[1080,512]{1,0:T(8,128)S(1)}) fusion(f32[512]{0:T(512)} %bitcast.780, bf16[1080,128]{1,0:T(8,128)(2,1)S(1)} %bitcast.741, bf16[2,128,512]{2,1,0:T(8,128)(2,1)} %param.19), kind=kOutput, calls=%fused_computation.116 | convolution fusion | flops 178053120 | bytes 3727360 | tf_op jit(solution)/shard_map/dot_general | solution.py:67
  85.7 1.9 convert_reduce_fusion
  93.1 5.3 collective-permute-start.9
  98.5 1.7 fusion.200
  100.4 2.2 collective-permute-start.10
  102.6 12.7 %collective-permute-start.11 = (bf16[3,30,128]{2,1,0:T(8,128)(2,1)S(1)}, bf16[3,30,128]{2,1,0:T(8,128)(2,1)S(1)}, u32[]{:S(2)}, u32[]{:S(2)}) collective-permute-start(bf16[3,30,128]{2,1,0:T(8,128)(2,1)S(1)} %get-tuple-element.200), channel_id=1, source_target_pairs={{0,1},{1,2},{2,3},{3,4},{4,5},{5,6},{6,7},{8,9},{9,10},{10,11},{11... | collective-permute-start | bytes 69128 | tf_op jit(solution)/shard_map/ppermute | solution.py:28
  115.8 4.9 stack.474
  122.0 6.2 multiply_convert_fusion.1
  128.5 1.9 convert_reduce_fusion.1
  137.0 2.4 multiply_reduce_fusion.1
  142.7 133.3 %all-reduce = (f32[2,7,7,128]{3,2,1,0:T(8,128)S(1)}, f32[2,128]{1,0:T(2,128)S(1)}, f32[2,128]{1,0:T(2,128)S(1)}, f32[2,128]{1,0:T(2,128)S(1)}, f32[2,512]{1,0:T(...) all-reduce(f32[2,7,7,128]{3,2,1,0:T(8,128)S(1)} %pad_maximum_fusion, ...), channel_id=1, replica_groups=mesh['lon'=32,'lat'=8] {'lon'}, use_global_device_ids=true, to_apply=%region_106.0 | all-reduce | flops 14848 | bytes 118784 | tf_op jit(solution)/shard_map/psum | solution.py:17
  276.0 33.0 %all-reduce.2 = (f32[2,7,7,128]{3,2,1,0:T(8,128)S(1)}, f32[2,128]{1,0:T(2,128)S(1)}, f32[2,128]{1,0:T(2,128)S(1)}, f32[2,128]{1,0:T(2,128)S(1)}, f32[2,512]{1,0:...) all-reduce(f32[2,7,7,128]{3,2,1,0:T(8,128)S(1)} %get-tuple-element., ...), channel_id=1, replica_groups=mesh['lon'=32,'lat'=8] {'lat'}, use_global_device_ids=true, to_apply=%region_107.0 | all-reduce | flops 14848 | bytes 118784 | tf_op jit(solution)/shard_map/psum | solution.py:17
  314.4 3.4 collective-permute-done.12
  317.9 4.2 collective-permute-start.14
  322.1 3.9 collective-permute-start.15
  328.0 259.8 %all-reduce.7.cloned.1.call-done = (f32[2,128,512]{2,1,0:T(8,128)}, f32[2,512,128]{2,1,0:T(8,128)}) async-done(((f32[2,128,512]{2,1,0:T(8,128)}, f32[2,512,128]{2,1,0:T(8,128)}), (f32[2,128,512]{2,1,0:T(8,128)}, f32[2,512,128]{2,1,0:T(8,128)})) %all-reduce.7.cloned.1.call-update) | async-done | bytes 1048592 | tf_op jit(solution)/shard_map/psum | solution.py:17
  588.1 5.8 fusion.280
  593.9 76.3 %all-reduce.9.cloned.1.call-done = (f32[2,128,512]{2,1,0:T(8,128)}, f32[2,512,128]{2,1,0:T(8,128)}) async-done(((f32[2,128,512]{2,1,0:T(8,128)}, f32[2,512,128]{2,1,0:T(8,128)}), (f32[2,128,512]{2,1,0:T(8,128)}, f32[2,512,128]{2,1,0:T(8,128)})) %all-reduce.9.cloned.1.call-update) | async-done | bytes 1048592 | tf_op jit(solution)/shard_map/psum | solution.py:17
  670.2 1.9 broadcast_multiply_fusion.1
  672.1 1.9 broadcast_multiply_fusion
  (472 shorter events, 43.9 us)
Async XLA Ops:
  7.2 580.6 %all-reduce.7.cloned.1.call-start = ((), (), s32[]{:S(2)}) async-start(), calls=%async_computation | async-start | bytes 2097152 | tf_op jit(solution)/shard_map/psum | solution.py:17
  8.2 20.2 %collective-permute-start = (bf16[45,3,128]{2,1,0:T(4,128)(2,1)S(1)}, bf16[45,3,128]{2,1,0:T(4,128)(2,1)S(1)}, u32[]{:S(2)}, u32[]{:S(2)}) collective-permute-start(bf16[45,3,128]{2,1,0:T(4,128)(2,1)S(1)} %get-tuple-element.216), channel_id=1, source_target_pairs={{0,8},{8,16},{16,24},{24,32},{32,40},{40,48},{48,56},{56,64},{64,7... | collective-permute-start | bytes 103688 | tf_op jit(solution)/shard_map/ppermute | solution.py:28
  8.3 20.1 %collective-permute-start.1 = (bf16[45,3,128]{2,1,0:T(4,128)(2,1)S(1)}, bf16[45,3,128]{2,1,0:T(4,128)(2,1)S(1)}, u32[]{:S(2)}, u32[]{:S(2)}) collective-permute-start(bf16[45,3,128]{2,1,0:T(4,128)(2,1)S(1)} %get-tuple-element.217), channel_id=1, source_target_pairs={{8,0},{16,8},{24,16},{32,24},{40,32},{48,40},{56,48},{64,56},{72,6... | collective-permute-start | bytes 103688 | tf_op jit(solution)/shard_map/ppermute | solution.py:29
  29.2 5.9 collective-permute-start.2
  32.6 5.7 collective-permute-start.3
  53.1 7.2 %collective-permute-start.4 = (bf16[45,3,128]{2,1,0:T(4,128)(2,1)S(1)}, bf16[45,3,128]{2,1,0:T(4,128)(2,1)S(1)}, u32[]{:S(2)}, u32[]{:S(2)}) collective-permute-start(bf16[45,3,128]{2,1,0:T(4,128)(2,1)S(1)} %get-tuple-element.214), channel_id=1, source_target_pairs={{0,8},{8,16},{16,24},{24,32},{32,40},{40,48},{48,56},{56,64},{64,7... | collective-permute-start | bytes 103688 | tf_op jit(solution)/shard_map/ppermute | solution.py:28
  53.2 7.1 %collective-permute-start.5 = (bf16[45,3,128]{2,1,0:T(4,128)(2,1)S(1)}, bf16[45,3,128]{2,1,0:T(4,128)(2,1)S(1)}, u32[]{:S(2)}, u32[]{:S(2)}) collective-permute-start(bf16[45,3,128]{2,1,0:T(4,128)(2,1)S(1)} %get-tuple-element.215), channel_id=1, source_target_pairs={{8,0},{16,8},{24,16},{32,24},{40,32},{48,40},{56,48},{64,56},{72,6... | collective-permute-start | bytes 103688 | tf_op jit(solution)/shard_map/ppermute | solution.py:29
  60.3 6.5 collective-permute-start.6
  63.4 6.4 collective-permute-start.7
  93.0 7.3 %collective-permute-start.8 = (bf16[45,3,128]{2,1,0:T(4,128)(2,1)S(1)}, bf16[45,3,128]{2,1,0:T(4,128)(2,1)S(1)}, u32[]{:S(2)}, u32[]{:S(2)}) collective-permute-start(bf16[45,3,128]{2,1,0:T(4,128)(2,1)S(1)} %get-tuple-element.212), channel_id=1, source_target_pairs={{0,8},{8,16},{16,24},{24,32},{32,40},{40,48},{48,56},{56,64},{64,7... | collective-permute-start | bytes 103688 | tf_op jit(solution)/shard_map/ppermute | solution.py:28
  93.1 7.2 %collective-permute-start.9 = (bf16[45,3,128]{2,1,0:T(4,128)(2,1)S(1)}, bf16[45,3,128]{2,1,0:T(4,128)(2,1)S(1)}, u32[]{:S(2)}, u32[]{:S(2)}) collective-permute-start(bf16[45,3,128]{2,1,0:T(4,128)(2,1)S(1)} %get-tuple-element.213), channel_id=1, source_target_pairs={{8,0},{16,8},{24,16},{32,24},{40,32},{48,40},{56,48},{64,56},{72,6... | collective-permute-start | bytes 103688 | tf_op jit(solution)/shard_map/ppermute | solution.py:29
  100.4 20.3 %collective-permute-start.10 = (bf16[3,30,128]{2,1,0:T(8,128)(2,1)S(1)}, bf16[3,30,128]{2,1,0:T(8,128)(2,1)S(1)}, u32[]{:S(2)}, u32[]{:S(2)}) collective-permute-start(bf16[3,30,128]{2,1,0:T(8,128)(2,1)S(1)} %get-tuple-element.199), channel_id=1, source_target_pairs={{1,0},{2,1},{3,2},{4,3},{5,4},{6,5},{7,6},{9,8},{10,9},{11,10},{12... | collective-permute-start | bytes 69128 | tf_op jit(solution)/shard_map/ppermute | solution.py:29
  102.6 18.2 %collective-permute-start.11 = (bf16[3,30,128]{2,1,0:T(8,128)(2,1)S(1)}, bf16[3,30,128]{2,1,0:T(8,128)(2,1)S(1)}, u32[]{:S(2)}, u32[]{:S(2)}) collective-permute-start(bf16[3,30,128]{2,1,0:T(8,128)(2,1)S(1)} %get-tuple-element.200), channel_id=1, source_target_pairs={{0,1},{1,2},{2,3},{3,4},{4,5},{5,6},{6,7},{8,9},{9,10},{10,11},{11... | collective-permute-start | bytes 69128 | tf_op jit(solution)/shard_map/ppermute | solution.py:28
  310.7 3.7 collective-permute-start.13
  310.7 7.1 %collective-permute-start.12 = (bf16[45,3,128]{2,1,0:T(4,128)(2,1)S(1)}, bf16[45,3,128]{2,1,0:T(4,128)(2,1)S(1)}, u32[]{:S(2)}, u32[]{:S(2)}) collective-permute-start(bf16[45,3,128]{2,1,0:T(4,128)(2,1)S(1)} %get-tuple-element.211), channel_id=1, source_target_pairs={{0,8},{8,16},{16,24},{24,32},{32,40},{40,48},{48,56},{56,64},{64,7... | collective-permute-start | bytes 103688 | tf_op jit(solution)/shard_map/ppermute | solution.py:28
  312.9 274.9 %copy-start.33 = (f32[128]{0:T(128)S(1)}, f32[128]{0:T(128)}, u32[]{:S(2)}) copy-start(f32[128]{0:T(128)} %copy-done.32) | copy-start | bytes 1540
  312.9 274.9 %copy-start.35 = (f32[128]{0:T(128)S(1)}, f32[128]{0:T(128)}, u32[]{:S(2)}) copy-start(f32[128]{0:T(128)} %copy-done.34) | copy-start | bytes 1540
  312.9 274.9 %copy-start.37 = (f32[128]{0:T(128)S(1)}, f32[128]{0:T(128)}, u32[]{:S(2)}) copy-start(f32[128]{0:T(128)} %copy-done.36) | copy-start | bytes 1540
  312.9 274.9 %copy-start.39 = (f32[128]{0:T(128)S(1)}, f32[128]{0:T(128)}, u32[]{:S(2)}) copy-start(f32[128]{0:T(128)} %copy-done.38) | copy-start | bytes 1540
  312.9 274.9 %copy-start.41 = (f32[128]{0:T(128)S(1)}, f32[128]{0:T(128)}, u32[]{:S(2)}) copy-start(f32[128]{0:T(128)} %copy-done.40) | copy-start | bytes 1540
  313.0 274.9 %copy-start.43 = (f32[128]{0:T(128)S(1)}, f32[128]{0:T(128)}, u32[]{:S(2)}) copy-start(f32[128]{0:T(128)} %copy-done.42) | copy-start | bytes 1540
  313.0 274.9 %copy-start.45 = (f32[128]{0:T(128)S(1)}, f32[128]{0:T(128)}, u32[]{:S(2)}) copy-start(f32[128]{0:T(128)} %copy-done.44) | copy-start | bytes 1540
  313.0 274.9 %copy-start.47 = (f32[128]{0:T(128)S(1)}, f32[128]{0:T(128)}, u32[]{:S(2)}) copy-start(f32[128]{0:T(128)} %copy-done.46) | copy-start | bytes 1540
  313.0 274.9 %copy-start.49 = (f32[128]{0:T(128)S(1)}, f32[128]{0:T(128)}, u32[]{:S(2)}) copy-start(f32[128]{0:T(128)} %copy-done.48) | copy-start | bytes 1540
  313.0 274.9 %copy-start.51 = (f32[128]{0:T(128)S(1)}, f32[128]{0:T(128)}, u32[]{:S(2)}) copy-start(f32[128]{0:T(128)} %copy-done.50) | copy-start | bytes 1540
  313.0 274.9 %copy-start.53 = (f32[128]{0:T(128)S(1)}, f32[128]{0:T(128)}, u32[]{:S(2)}) copy-start(f32[128]{0:T(128)} %copy-done.52) | copy-start | bytes 1540
  313.0 274.9 %copy-start.55 = (f32[128]{0:T(128)S(1)}, f32[128]{0:T(128)}, u32[]{:S(2)}) copy-start(f32[128]{0:T(128)} %copy-done.54) | copy-start | bytes 1540
  313.0 274.9 %copy-start.57 = (f32[128]{0:T(128)S(1)}, f32[128]{0:T(128)}, u32[]{:S(2)}) copy-start(f32[128]{0:T(128)} %copy-done.56) | copy-start | bytes 1540
  313.0 274.9 %copy-start.59 = (f32[128]{0:T(128)S(1)}, f32[128]{0:T(128)}, u32[]{:S(2)}) copy-start(f32[128]{0:T(128)} %copy-done.58) | copy-start | bytes 1540
  313.3 356.9 %all-reduce.9.cloned.1.call-start = ((), (), s32[]{:S(2)}) async-start(), calls=%async_computation.1 | async-start | bytes 2097152 | tf_op jit(solution)/shard_map/psum | solution.py:17
  317.9 9.4 %collective-permute-start.14 = (bf16[3,30,128]{2,1,0:T(8,128)(2,1)S(1)}, bf16[3,30,128]{2,1,0:T(8,128)(2,1)S(1)}, u32[]{:S(2)}, u32[]{:S(2)}) collective-permute-start(bf16[3,30,128]{2,1,0:T(8,128)(2,1)S(1)} %get-tuple-element.195), channel_id=1, source_target_pairs={{1,0},{2,1},{3,2},{4,3},{5,4},{6,5},{7,6},{9,8},{10,9},{11,10},{12... | collective-permute-start | bytes 69128 | tf_op jit(solution)/shard_map/ppermute | solution.py:29
  322.1 5.7 collective-permute-start.15
  (172 other events, 8468.5 us)
Sparse Core Ops, SparseCore 0:
  313.4 274.3 all-reduce.6
  590.6 79.5 all-reduce.8
